TPU v7x, 32 devices: a whole 2x2x4 slice. The times are simulated.
32 devices in a mesh: tp: 2 (over y), req: 16 (over z, x, core).
Axes of the slice: x: 2, y: 2, z: 4, core: 2. Of those that a mesh axis runs over, the one named last changes fastest.
Arguments:
- token_ids: int32 [8192], P('req'), may hold values from 0 to 31999, as said below
- prompt_lengths: int32 [16, 4], P('req'), may hold values from 1 to 256, 512 in all within a row
- tenant_ids: int32 [16, 4], P('req'), may hold values from 0 to 1, never falling along the last dimension, each value on 1 to 3 neighbouring positions
- embed_table: bfloat16 [32000, 1536], P('req'), may hold values from -6 to 6
- attention_gain: float32 [1536], replicated, may hold values from 0.1 to 1.9
- qkv_weight: float32 [1536, 3072], P(('tp', 'req')), may hold values from -0.25 to 0.25
- out_weight: bfloat16 [1536, 1536], P('tp'), may hold values from -0.15625 to 0.15625
- ffn_gain: float32 [1536], replicated, may hold values from 0.1 to 1.9
- gate_up_weight: float32 [1536, 8192], P(('tp', 'req')), may hold values from -0.15625 to 0.15625
- down_weight: bfloat16 [4096, 1536], P('tp'), may hold values from -0.09375 to 0.09375
Outputs:
- final_hidden: bfloat16 [8192, 1536], P('req')
- kv_cache: bfloat16 [2, 8192, 768], P(None, 'req', 'tp')
Inputs may be any that keep to these rules, and one draw needn't show every extreme that they name: Split token_ids into aligned blocks of 256 tokens and the ids into ranges of 2000 consecutive ids: no block has more than 32 ids in one range, and one range gets exactly 32 ids from every block. `prompt_lengths`: the 4 lengths of a request group sum to 512. `tenant_ids`: never falling along the prompts of a request group; every tenant has one to 3 prompts.
All inputs are finite; a program needn't handle non-finite values.
Results may differ from a plain program's by a relative error of at most 0.01.
Values may be sent and summed in bfloat16 or wider, within the bound.
No kernel may reach another device: no remote copies, remote signals or barrier semaphores. Data moves between devices by JAX's collectives and lax.ppermute only.
A program may use at most 128 MiB of HBM per device.

v0:
```python
import jax
import jax.numpy as jnp
from jax import lax
from jax.sharding import PartitionSpec as P

HEAD_DIM = 96
rope_base = 100000.0
norm_eps = 1e-05


def rms_scaled(values, gain):
    mean_square = jnp.mean(values * values, axis=-1, keepdims=True)
    return (values * lax.rsqrt(mean_square + norm_eps) * gain).astype(jnp.bfloat16)


def token_layout(lengths, tenants, row_count):
    positions = jnp.arange(row_count, dtype=jnp.int32)
    prompt_ends = jnp.cumsum(lengths)
    prompt_starts = prompt_ends - lengths
    passed = (positions[:, None] >= prompt_ends[None, :]).astype(jnp.int32)
    prompt = jnp.sum(passed, axis=1)
    in_prompt = (prompt[:, None] == jnp.arange(lengths.shape[0], dtype=jnp.int32)[None, :]).astype(
        jnp.int32
    )
    offset = positions - jnp.sum(in_prompt * prompt_starts[None, :], axis=1)
    tenant = jnp.sum(in_prompt * tenants[None, :], axis=1)
    return (offset, tenant)


def rotate(values, offset):
    half_dim = values.shape[-1] // 2
    frequency = rope_base ** (-2.0 * jnp.arange(half_dim, dtype=jnp.float32) / values.shape[-1])
    angles = offset.astype(jnp.float32)[:, None] * frequency[None, :]
    cosine = jnp.cos(angles)[:, None, :]
    sine_part = jnp.sin(angles)[:, None, :]
    lower_half = values[..., :half_dim]
    upper_half = values[..., half_dim:]
    return jnp.concatenate(
        [
            lower_half * cosine - upper_half * sine_part,
            upper_half * cosine + lower_half * sine_part,
        ],
        axis=-1,
    )


def attend(queries, key_heads, value_heads, tenant):
    row_count = queries.shape[0]
    positions = jnp.arange(row_count, dtype=jnp.int32)
    score_scale = queries.shape[-1] ** (-0.5)
    allowed = (positions[None, :] <= positions[:, None]) & (tenant[None, :] == tenant[:, None])
    scores = (
        jnp.einsum("qkgd,skd->kgqs", queries, key_heads, preferred_element_type=jnp.float32)
        * score_scale
    )
    scores = jnp.where(allowed[None, None], scores, -jnp.inf)
    row_max = jnp.max(scores, axis=-1, keepdims=True)
    expo = jnp.exp(scores - row_max)
    weights = (expo / jnp.sum(expo, axis=-1, keepdims=True)).astype(jnp.bfloat16)
    mixed_out = jnp.einsum(
        "kgqs,skd->qkgd", weights, value_heads, preferred_element_type=jnp.float32
    )
    pieces = mixed_out.astype(jnp.bfloat16)
    return pieces


def ffn_hidden(normed_ffn, gate_cols, ff_half):
    gate_up = jnp.dot(normed_ffn, gate_cols, preferred_element_type=jnp.float32)
    return (jax.nn.silu(gate_up[:, :ff_half]) * gate_up[:, ff_half:]).astype(jnp.bfloat16)


def per_device(
    token_ids,
    prompt_lengths,
    tenant_ids,
    embed_table,
    attention_gain,
    qkv_weight,
    out_weight,
    ffn_gain,
    gate_up_weight,
    down_weight,
):
    tp_count = lax.axis_size("tp")
    tp_index = lax.axis_index("tp")
    group_count = lax.axis_size("req")
    tokens = token_ids.shape[0]
    looked = tokens // tp_count
    own_rows = embed_table.shape[0]
    capacity = max(2, 2 * looked // group_count)
    my_ids = lax.dynamic_slice_in_dim(token_ids, tp_index * looked, looked)
    owner_of = my_ids // own_rows
    row_in_range = my_ids - owner_of * own_rows
    owner_hits = (owner_of[:, None] == jnp.arange(group_count, dtype=jnp.int32)[None, :]).astype(
        jnp.int32
    )
    slot_of = jnp.sum((jnp.cumsum(owner_hits, axis=0) - owner_hits) * owner_hits, axis=1)
    requests = (
        jnp.full((group_count, capacity), -1, jnp.int32).at[owner_of, slot_of].set(row_in_range)
    )
    found_rows = jnp.take(
        embed_table,
        jnp.maximum(lax.all_to_all(requests, "req", split_axis=0, concat_axis=0, tiled=True), 0),
        axis=0,
    )
    returned = lax.all_to_all(found_rows, "req", split_axis=0, concat_axis=0, tiled=True)
    embedded = lax.all_gather(returned[owner_of, slot_of], "tp", axis=0, tiled=True)
    offset, tenant = token_layout(prompt_lengths[0], tenant_ids[0], tokens)
    rows_here = qkv_weight.shape[0]
    q_half = out_weight.shape[0]
    ff_half = down_weight.shape[0]
    q_full = q_half * tp_count
    kv_half = (qkv_weight.shape[1] - q_full) // (2 * tp_count)
    kv_full = kv_half * tp_count
    packed = qkv_weight.astype(jnp.bfloat16)
    gate_up_bf = gate_up_weight.astype(jnp.bfloat16)
    packed_rows = jnp.concatenate(
        [
            packed[:, :q_full].reshape(rows_here, tp_count, q_half),
            packed[:, q_full : q_full + kv_full].reshape(rows_here, tp_count, kv_half),
            packed[:, q_full + kv_full :].reshape(rows_here, tp_count, kv_half),
            gate_up_bf.reshape(rows_here, 2, tp_count, ff_half)
            .transpose(0, 2, 1, 3)
            .reshape(rows_here, tp_count, 2 * ff_half),
        ],
        axis=2,
    )
    collected = lax.all_gather(packed_rows, "req", axis=0, tiled=True)
    columns = lax.all_to_all(collected, "tp", split_axis=1, concat_axis=0, tiled=True)
    weights = columns[:, 0, :]
    normed = rms_scaled(embedded.astype(jnp.float32), attention_gain)
    projected = jnp.dot(
        normed, weights[:, : q_half + 2 * kv_half], preferred_element_type=jnp.float32
    )
    kv_local = kv_half // HEAD_DIM
    queries = rotate(
        projected[:, :q_half].reshape(tokens, q_half // HEAD_DIM, HEAD_DIM), offset
    ).astype(jnp.bfloat16)
    key_heads = rotate(
        projected[:, q_half : q_half + kv_half].reshape(tokens, kv_local, HEAD_DIM), offset
    ).astype(jnp.bfloat16)
    value_heads = (
        projected[:, q_half + kv_half :].reshape(tokens, kv_local, HEAD_DIM).astype(jnp.bfloat16)
    )
    kv_cache = jnp.stack([key_heads.reshape(tokens, kv_half), value_heads.reshape(tokens, kv_half)])
    attended = attend(
        queries.reshape(tokens, kv_local, -1, HEAD_DIM), key_heads, value_heads, tenant
    ).reshape(tokens, q_half)
    gate_cols = weights[:, q_half + 2 * kv_half :]
    attn_sum = lax.psum(
        jnp.dot(attended, out_weight, preferred_element_type=jnp.float32).astype(jnp.bfloat16), "tp"
    ).astype(jnp.float32)
    residual = embedded.astype(jnp.float32) + attn_sum
    normed_ffn = rms_scaled(residual, ffn_gain)
    hidden = ffn_hidden(normed_ffn, gate_cols, ff_half)
    ffn_sum = lax.psum(
        jnp.dot(hidden, down_weight, preferred_element_type=jnp.float32).astype(jnp.bfloat16), "tp"
    ).astype(jnp.float32)
    final_out = (residual + ffn_sum).astype(jnp.bfloat16)
    return (final_out, kv_cache)


def solution(mesh):
    return jax.shard_map(
        per_device,
        mesh=mesh,
        in_specs=(
            P("req"),
            P("req", None),
            P("req", None),
            P("req", None),
            P(),
            P(("tp", "req"), None),
            P("tp", None),
            P(),
            P(("tp", "req"), None),
            P("tp", None),
        ),
        out_specs=(P("req", None), P(None, "req", "tp")),
        check_vma=False,
    )
```

profile of v0, /device:TPU:0, one launch (start us, length us, event | category | flops | bytes accessed | tf_op | source)
XLA Modules:
  0.0 530.0 jit_solution(3900098590027576408)
XLA Ops:
  8.1 1.2 convert_element_type.91
  9.3 2.4 convert_element_type.92
  11.7 2.6 reshape.236
  14.3 1.5 copy.85
  15.8 2.5 reshape.237
  18.4 1.1 pad_maximum_fusion
  19.5 0.1 multiply_subtract_fusion.1
  19.6 0.6 reduce-window.10
  20.1 0.2 slice_reduce_fusion
  20.4 0.1 fusion.31
  20.5 12.8 %scatter_fusion = s32[16,32]{1,0:T(8,128)S(1)} fusion(s32[16,32]{1,0:T(8,128)S(1)} %broadcast_in_dim.22, s32[256]{0:T(256)S(1)} %bitcast.107, s32[256]{0:T(256)S(1)} %get-tuple-element.4), kind=kCustom, calls=%fused_computation.2 | custom fusion | bytes 5120 | tf_op jit(solution)/shard_map/scatter | solution.py:99
  33.3 13.7 %all_to_all.29 = s32[16,1,32]{2,1,0:T(1,128)S(1)} all-to-all(s32[16,1,32]{2,1,0:T(1,128)S(1)} %bitcast.105), channel_id=1, replica_groups=mesh['tp'=2,'req'=16] {'req'}, dimensions={0} | all-to-all | bytes 4096 | tf_op jit(solution)/shard_map/all_to_all | solution.py:103
  47.0 8.0 %gather_fusion = bf16[512,1536]{1,0:T(8,128)(2,1)} fusion(bf16[2000,1536]{1,0:T(8,128)(2,1)} %param.13, s32[1024]{0:T(1024)S(1)} %pad_clamp_fusion), kind=kCustom, calls=%fused_computation | custom fusion | bytes 3147776 | tf_op jit(solution)/shard_map/jit(_take)/gather | solution.py:101
  55.0 1.7 broadcast_select_fusion
  56.7 60.0 %all_to_all.30 = bf16[16,32,1536]{2,1,0:T(8,128)(2,1)} all-to-all(bf16[16,32,1536]{2,1,0:T(8,128)(2,1)S(1)} %broadcast_select_fusion), channel_id=1, replica_groups=mesh['tp'=2,'req'=16] {'req'}, dimensions={0} | all-to-all | bytes 3145728 | tf_op jit(solution)/shard_map/all_to_all | solution.py:106
  116.7 25.0 %all-gather.5.cloned.1.call-done = bf16[768,2,5632]{2,0,1:T(8,128)(2,1)} async-done(((bf16[48,2,5632]{2,0,1:T(8,128)(2,1)}), bf16[768,2,5632]{2,0,1:T(8,128)(2,1)}) %all-gather.5.cloned.1.call-update) | async-done | bytes 17301520 | tf_op jit(solution)/shard_map/all_gather | solution.py:128
  141.7 9.8 %all-to-all-start.2 = ((bf16[768,2,5632]{2,0,1:T(8,128)(2,1)}), bf16[768,2,5632]{2,0,1:T(8,128)(2,1)}, u32[]{:S(2)}, u32[]{:S(2)}) async-start(bf16[768,2,5632]{2,0,1:T(8,128)(2,1)} %all-gather.5.cloned.1.call-done), calls=%async_computation.2 | async-start | bytes 34603008 | tf_op jit(solution)/shard_map/all_to_all | solution.py:129
  151.6 4.6 gather_fusion.1
  156.3 0.2 all-reduce.3.cloned.1.call-start
  156.5 0.2 reduce-window.14
  156.8 0.1 select_reduce_fusion
  156.9 1.1 multiply_cosine_fusion
  158.0 0.9 fusion.21
  158.9 47.1 %all-gather.3.cloned.1.call-done = bf16[512,1536]{1,0:T(8,128)(2,1)} async-done(((bf16[256,1536]{1,0:T(8,128)(2,1)}), bf16[512,1536]{1,0:T(8,128)(2,1)}) %all-gather.3.cloned.1.call-update) | async-done | bytes 1572880 | tf_op jit(solution)/shard_map/all_gather | solution.py:107
  206.0 1.8 fusion.11
  207.8 149.1 %all-to-all-done.2 = bf16[768,2,5632]{2,0,1:T(8,128)(2,1)} async-done(((bf16[768,2,5632]{2,0,1:T(8,128)(2,1)}), bf16[768,2,5632]{2,0,1:T(8,128)(2,1)}, u32[]{:S(2)}, u32[]{:S(2)}) %all-to-all-start.2) | async-done | bytes 17301536 | tf_op jit(solution)/shard_map/all_to_all | solution.py:129
  356.9 5.0 fusion.4
  362.0 1.4 slice.79
  363.4 0.8 copy-done.3
  364.2 0.9 copy.68
  365.1 3.1 copy.70
  368.3 1.1 copy.69
  369.5 2.4 subtract_convert_fusion
  371.8 1.2 multiply_subtract_fusion
  373.1 7.4 %fusion.44 = (f32[4,2,512]{2,1,0:T(2,128)S(1)}, f32[4,2,512,512]{2,3,1,0:T(8,128)}) fusion(pred[512,512]{0,1:T(8,128)(4,1)} %fusion.21, bf16[512,4,2,48]{0,3,2,1:T(8,128)(2,1)} %bitcast.117, bf16[512,4,2,48]{0,3,2,1:T(8,128)(2,1)S(1)} %bitcast.116, bf16[512,4,48]{0,2,1:T(8,128)(2,1)S(1)} %get-tuple-element.11, bf16[512,4,48]{0,2,1:T(8,128)(2,1)S(1)} %get-tuple-element.10), kind=kOutput, calls=%fused_computation.93 | convolution fusion | flops 413401600 | bytes 9846784 | tf_op jit(solution)/shard_map/sub | solution.py:58
  380.5 4.2 fusion.20
  384.7 2.6 convolution_convert_fusion.1
  387.3 0.3 all-reduce.5.cloned.1.call-start
  387.6 55.3 %all-reduce.3.cloned.1.call-done = bf16[512,1536]{1,0:T(8,128)(2,1)} async-done(((bf16[512,1536]{1,0:T(8,128)(2,1)}), bf16[512,1536]{1,0:T(8,128)(2,1)}) %all-reduce.3.cloned.1.call-update) | async-done | bytes 1572880 | tf_op jit(solution)/shard_map/psum | solution.py:150
  442.9 2.6 multiply_reduce_fusion
  445.5 0.2 copy-done.2
  445.7 12.1 %fusion.1 = f32[512,4096]{1,0:T(8,128)} fusion(bf16[1536,5632]{1,0:T(8,128)(2,1)} %bitcast.14, bf16[512,1536]{1,0:T(8,128)(2,1)S(1)} %copy-done.2, bf16[512,1536]{1,0:T(8,128)(2,1)S(1)} %copy-done.1, f32[1536]{0:T(1024)S(1)} %copy-done.10, f32[512]{0:T(512)S(1)} %add_rsqrt_fusion), kind=kOutput, calls=%fused_computation.4 | convolution fusion | flops 6447169536 | bytes 24125440 | tf_op jit(solution)/shard_map/dot_general | solution.py:68
  457.8 9.1 %convolution_convert_fusion = bf16[512,1536]{1,0:T(8,128)(2,1)} fusion(bf16[2048,1536]{1,0:T(8,128)(2,1)S(1)} %bitcast.129, f32[512,4096]{1,0:T(8,128)} %fusion.1), kind=kOutput, calls=%fused_computation.27 | convolution fusion | flops 3228303360 | bytes 16252928 | tf_op jit(solution)/shard_map/dot_general | solution.py:157
  467.0 0.2 copy.72
  467.2 1.2 slice_bitcast_fusion
  468.4 1.0 pad_maximum_fusion.2
  469.4 49.0 %all-reduce.5.cloned.1.call-done = bf16[512,1536]{1,0:T(8,128)(2,1)} async-done(((bf16[512,1536]{1,0:T(8,128)(2,1)}), bf16[512,1536]{1,0:T(8,128)(2,1)}) %all-reduce.5.cloned.1.call-update) | async-done | bytes 1572880 | tf_op jit(solution)/shard_map/psum | solution.py:156
  518.3 4.1 add_convert_fusion
  (57 shorter events, 0.6 us)
Async XLA Ops:
  8.0 376.7 %copy-start = (bf16[768,1536]{1,0:T(8,128)(2,1)S(1)}, bf16[768,1536]{1,0:T(8,128)(2,1)}, u32[]{:S(2)}) copy-start(bf16[768,1536]{1,0:T(8,128)(2,1)} %param.16) | copy-start | bytes 7077892
  8.0 133.7 %all-gather.5.cloned.1.call-start = ((), (), s32[]{:S(2)}) async-start(), calls=%async_computation.4 | async-start | bytes 18382848 | tf_op jit(solution)/shard_map/all_gather | solution.py:128
  14.3 5.2 copy-start.8
  141.7 215.2 %all-to-all-start.2 = ((bf16[768,2,5632]{2,0,1:T(8,128)(2,1)}), bf16[768,2,5632]{2,0,1:T(8,128)(2,1)}, u32[]{:S(2)}, u32[]{:S(2)}) async-start(bf16[768,2,5632]{2,0,1:T(8,128)(2,1)} %all-gather.5.cloned.1.call-done), calls=%async_computation.2 | async-start | bytes 34603008 | tf_op jit(solution)/shard_map/all_to_all | solution.py:129
  151.5 54.5 %all-gather.3.cloned.1.call-start = ((), (), s32[]{:S(2)}) async-start(), calls=%async_computation.3 | async-start | bytes 2359296 | tf_op jit(solution)/shard_map/all_gather | solution.py:107
  151.6 4.9 copy-start.11
  151.6 5.2 copy-start.7
  151.6 205.3 %copy-start.9 = (f32[1536]{0:T(1024)S(1)}, f32[1536]{0:T(1024)}, u32[]{:S(2)}) copy-start(f32[1536]{0:T(1024)} %param.14) | copy-start | bytes 18436
  156.3 286.6 %all-reduce.3.cloned.1.call-start = ((), (), s32[]{:S(2)}) async-start(), calls=%async_computation.5 | async-start | bytes 3145728 | tf_op jit(solution)/shard_map/psum | solution.py:150
  362.0 2.2 copy-start.3
  364.2 4.1 slice-start
  365.1 4.3 copy-start.4
  365.1 4.3 copy-start.5
  373.1 7.4 %copy-start.6 = (bf16[512,384]{0,1:T(8,128)(2,1)S(1)}, bf16[512,384]{0,1:T(8,128)(2,1)}, u32[]{:S(2)}) copy-start(bf16[512,384]{0,1:T(8,128)(2,1)} %copy.68) | copy-start | bytes 1179652
  387.3 58.3 %copy-start.10 = (f32[1536]{0:T(1024)S(1)}, f32[1536]{0:T(1024)}, u32[]{:S(2)}) copy-start(f32[1536]{0:T(1024)} %param.17) | copy-start | bytes 18436
  387.3 131.0 %all-reduce.5.cloned.1.call-start = ((), (), s32[]{:S(2)}) async-start(), calls=%async_computation.6 | async-start | bytes 3145728 | tf_op jit(solution)/shard_map/psum | solution.py:156
  442.9 2.6 copy-start.1
  442.9 2.8 copy-start.2
  442.9 14.9 %slice-start.1 = ((s8[6291456]{0:T(1024)(128)(4,1)}), s8[4194304]{0:T(1024)(128)(4,1)S(1)}, s32[]{:S(2)}) async-start(s8[6291456]{0:T(1024)(128)(4,1)} %bitcast.128), calls=%async_computation.8 | async-start | bytes 8388608
  445.7 12.1 %slice-start.2 = ((s8[6291456]{0:T(1024)(128)(4,1)}), s8[2097152]{0:T(1024)(128)(4,1)S(1)}, s32[]{:S(2)}) async-start(s8[6291456]{0:T(1024)(128)(4,1)} %bitcast.128), calls=%async_computation.9 | async-start | bytes 4194304
Sparse Core Ops, SparseCore 0:
  19.6 122.0 all-gather.4
Sparse Core Ops, SparseCore 1:
  156.4 49.6 all-gather.2
  387.4 55.5 all-reduce.2
  467.0 51.2 all-reduce.4
where the time goes:
time: 531 us; the launch traced here: 530 us
  waiting for transfers between devices  325 us (61%)
  blocking collectives  73.7 us (14%)
  local copies, waits for them, and re-layouts  41.4 us (8%)
  matrix products  40.4 us (8%)
  other arithmetic  22.7 us (4%)
  between operations  15.9 us (3%)
  starting transfers between devices  10.4 us (2%)
    all_to_all x1, waiting for transfers between devices, per_device(): lax.all_to_all(collected, 'tp', split_axis=1, concat_axis=0, tiled=True)  149 us
    all_to_all x1, blocking collectives, per_device(): lax.all_to_all(found_rows, 'req', split_axis=0, concat_axis=0, tiled=True)  60 us
    psum x1, waiting for transfers between devices, per_device(): lax.psum(jnp.dot(attended, out_weight, preferred_element_type=jnp.float32...  55.3 us
    psum x1, waiting for transfers between devices, per_device(): lax.psum(jnp.dot(hidden, down_weight, preferred_element_type=jnp.float32)...  49 us
    all_gather x1, waiting for transfers between devices, per_device(): lax.all_gather(returned[owner_of, slot_of], 'tp', axis=0, tiled=True)  47.1 us
    all_gather x1, waiting for transfers between devices, per_device(): collected = lax.all_gather(packed_rows, 'req', axis=0, tiled=True)  25 us
    all_to_all x1, blocking collectives, per_device(): lax.all_to_all(requests, 'req', split_axis=0, concat_axis=0, tiled=True)  13.7 us
    scatter x1, local copies, waits for them, and re-layouts, per_device(): jnp.full((group_count, capacity), -1, jnp.int32).at[owner_of, slot_of]  12.8 us
  transfers between devices with their start and end apart: 5, of which 5 were waited for; matrix products, arithmetic and copies ran while one was open for 7% of the time, Pallas kernels for 0%

commit v1 on v0

--- a/solution.py
+++ b/solution.py
@@ -1,3 +1,4 @@
+import functools
 import jax
 import jax.numpy as jnp
 from jax import lax
@@ -6,6 +7,43 @@
 HEAD_DIM = 96
 rope_base = 100000.0
 norm_eps = 1e-05
+
+
+def perform_unit_over_axis(my_data, d_out, xx):
+    clean = my_data.shape
+    out_arr = my_data.reshape(*clean[:d_out], xx, clean[d_out] // xx, *clean[d_out + 1 :])
+    main = jnp.moveaxis(out_arr, d_out, 0)
+    return main
+
+
+def direct_members_all(shard_in, in_dim):
+    shard_in = jnp.moveaxis(shard_in, 0, in_dim)
+    x_next = shard_in.shape
+    left_arr = shard_in.reshape(
+        *x_next[:in_dim], x_next[in_dim] * x_next[in_dim + 1], *x_next[in_dim + 2 :]
+    )
+    return left_arr
+
+
+def track_tracks_up(u_in, array_in, vals, bus_axis):
+    step_out = jax.lax.axis_size(bus_axis)
+    local_now, seen_now = (step_out, jax.lax.axis_index(bus_axis))
+    k_now = perform_unit_over_axis(u_in, array_in, local_now)
+    y_new = k_now
+    jj = 1
+    while jj < local_now:
+        upper, moved = ((seen_now + jj) % local_now, (seen_now - jj) % local_now)
+        built = lax.dynamic_index_in_dim(k_now, upper, 0)
+        reply = jax.lax.ppermute(
+            built, bus_axis, [(u, (u + jj) % local_now) for u in range(local_now)]
+        )
+        y_new = lax.dynamic_update_slice_in_dim(y_new, reply, moved, axis=0)
+        jj += 1
+    h_now = direct_members_all(y_new, vals)
+    return h_now
+
+
+check_the_sizes = functools.partial(track_tracks_up, array_in=0, vals=0, bus_axis="req")
 
 
 def rms_scaled(values, gain):
@@ -98,11 +136,7 @@
     requests = (
         jnp.full((group_count, capacity), -1, jnp.int32).at[owner_of, slot_of].set(row_in_range)
     )
-    found_rows = jnp.take(
-        embed_table,
-        jnp.maximum(lax.all_to_all(requests, "req", split_axis=0, concat_axis=0, tiled=True), 0),
-        axis=0,
-    )
+    found_rows = jnp.take(embed_table, jnp.maximum(check_the_sizes(requests), 0), axis=0)
     returned = lax.all_to_all(found_rows, "req", split_axis=0, concat_axis=0, tiled=True)
     embedded = lax.all_gather(returned[owner_of, slot_of], "tp", axis=0, tiled=True)
     offset, tenant = token_layout(prompt_lengths[0], tenant_ids[0], tokens)

time: 531 us -> 531 us (level)
  starting transfers between devices: 10.4 us -> 35 us
  waiting for transfers between devices: 325 us -> 311 us
  blocking collectives: 73.7 us -> 62.3 us
    ppermute x0 -> x15, starting transfers between devices: none -> 24.5 us  [track_tracks_up(): jax.lax.ppermute(built, bus_axis, [(u, (u + jj) % local_now) for u in ran...]
    all_gather x1, waiting for transfers between devices: 25 us -> 9.8 us  [per_device(): collected = lax.all_gather(packed_rows, 'req', axis=0, tiled=True)]
    all_to_all x1 -> x0, blocking collectives: 13.7 us -> none  [per_device(): lax.all_to_all(requests, 'req', split_axis=0, concat_axis=0, tiled=True)]
  transfers between devices with their start and end apart: 5 -> 20, of which waited for: 5 -> 6; matrix products, arithmetic and copies ran while one was open for 7% -> 7% of each run, Pallas kernels for 0% -> 0%
where the time goes in v1:
time: 531 us; the launch traced here: 530 us
  waiting for transfers between devices  311 us (59%)
  blocking collectives  62.3 us (12%)
  local copies, waits for them, and re-layouts  42 us (8%)
  matrix products  40.3 us (8%)
  starting transfers between devices  35 us (7%)
  other arithmetic  22.6 us (4%)
  between operations  16.2 us (3%)
    all_to_all x1, waiting for transfers between devices, per_device(): lax.all_to_all(collected, 'tp', split_axis=1, concat_axis=0, tiled=True)  149 us
    all_to_all x1, blocking collectives, per_device(): lax.all_to_all(found_rows, 'req', split_axis=0, concat_axis=0, tiled=True)  62.3 us
    psum x1, waiting for transfers between devices, per_device(): lax.psum(jnp.dot(attended, out_weight, preferred_element_type=jnp.float32...  55.3 us
    psum x1, waiting for transfers between devices, per_device(): lax.psum(jnp.dot(hidden, down_weight, preferred_element_type=jnp.float32)...  49 us
    all_gather x1, waiting for transfers between devices, per_device(): lax.all_gather(returned[owner_of, slot_of], 'tp', axis=0, tiled=True)  47.1 us
    ppermute x15, starting transfers between devices, track_tracks_up(): jax.lax.ppermute(built, bus_axis, [(u, (u + jj) % local_now) for u in ran...  24.5 us
    scatter x1, local copies, waits for them, and re-layouts, per_device(): jnp.full((group_count, capacity), -1, jnp.int32).at[owner_of, slot_of]  12.8 us
    dot_general x1, matrix products, ffn_hidden(): gate_up = jnp.dot(normed_ffn, gate_cols, preferred_element_type=jnp.float32)  12 us
  transfers between devices with their start and end apart: 20, of which 6 were waited for; matrix products, arithmetic and copies ran while one was open for 7% of the time, Pallas kernels for 0%

profile of v1, /device:TPU:0, one launch (start us, length us, event | category | flops | bytes accessed | tf_op | source)
XLA Modules:
  0.0 529.9 jit_solution(1350788178939315881)
XLA Ops:
  8.1 1.2 convert_element_type.91
  9.3 2.4 convert_element_type.92
  11.7 2.6 reshape.310
  14.3 1.5 copy.60
  15.8 2.5 reshape.311
  18.4 1.1 pad_maximum_fusion
  20.7 12.8 %scatter_fusion = s32[16,32]{1,0:T(8,128)S(1)} fusion(s32[16,32]{1,0:T(8,128)S(1)} %broadcast_in_dim.24, s32[256]{0:T(256)S(1)} %bitcast.143, s32[256]{0:T(256)S(1)} %get-tuple-element.4), kind=kCustom, calls=%fused_computation.2 | custom fusion | bytes 5120 | tf_op jit(solution)/shard_map/scatter | solution.py:137
  34.1 2.6 collective-permute-start.1
  36.7 2.4 collective-permute-start.2
  39.1 1.6 collective-permute-start.3
  40.8 1.2 collective-permute-start.5
  42.1 4.4 collective-permute-start.6
  47.3 2.4 collective-permute-start.9
  49.7 2.9 collective-permute-start.10
  52.7 1.9 collective-permute-start.11
  54.7 1.5 collective-permute-start.13
  56.2 2.3 collective-permute-start.14
  58.6 1.1 collective-permute-done.14
  59.9 8.1 %gather_fusion = bf16[512,1536]{1,0:T(8,128)(2,1)} fusion(bf16[2000,1536]{1,0:T(8,128)(2,1)} %param.13, s32[1024]{0:T(1024)S(1)} %pad_clamp_fusion), kind=kCustom, calls=%fused_computation | custom fusion | bytes 3147776 | tf_op jit(solution)/shard_map/jit(_take)/gather | solution.py:139
  68.0 1.6 broadcast_select_fusion
  69.6 62.3 %all_to_all.20 = bf16[16,32,1536]{2,1,0:T(8,128)(2,1)} all-to-all(bf16[16,32,1536]{2,1,0:T(8,128)(2,1)S(1)} %broadcast_select_fusion), channel_id=1, replica_groups=mesh['tp'=2,'req'=16] {'req'}, dimensions={0} | all-to-all | bytes 3145728 | tf_op jit(solution)/shard_map/all_to_all | solution.py:140
  131.9 9.8 %all-gather.5.cloned.1.call-done = bf16[768,2,5632]{2,0,1:T(8,128)(2,1)} async-done(((bf16[48,2,5632]{2,0,1:T(8,128)(2,1)}), bf16[768,2,5632]{2,0,1:T(8,128)(2,1)}) %all-gather.5.cloned.1.call-update) | async-done | bytes 17301520 | tf_op jit(solution)/shard_map/all_gather | solution.py:162
  141.7 9.9 %all-to-all-start.1 = ((bf16[768,2,5632]{2,0,1:T(8,128)(2,1)}), bf16[768,2,5632]{2,0,1:T(8,128)(2,1)}, u32[]{:S(2)}, u32[]{:S(2)}) async-start(bf16[768,2,5632]{2,0,1:T(8,128)(2,1)} %all-gather.5.cloned.1.call-done), calls=%async_computation.1 | async-start | bytes 34603008 | tf_op jit(solution)/shard_map/all_to_all | solution.py:163
  151.8 4.7 gather_fusion.1
  157.0 1.1 multiply_cosine_fusion
  158.1 0.9 fusion.21
  159.0 47.1 %all-gather.3.cloned.1.call-done = bf16[512,1536]{1,0:T(8,128)(2,1)} async-done(((bf16[256,1536]{1,0:T(8,128)(2,1)}), bf16[512,1536]{1,0:T(8,128)(2,1)}) %all-gather.3.cloned.1.call-update) | async-done | bytes 1572880 | tf_op jit(solution)/shard_map/all_gather | solution.py:141
  206.1 1.8 fusion.11
  207.9 149.1 %all-to-all-done.1 = bf16[768,2,5632]{2,0,1:T(8,128)(2,1)} async-done(((bf16[768,2,5632]{2,0,1:T(8,128)(2,1)}), bf16[768,2,5632]{2,0,1:T(8,128)(2,1)}, u32[]{:S(2)}, u32[]{:S(2)}) %all-to-all-start.1) | async-done | bytes 17301536 | tf_op jit(solution)/shard_map/all_to_all | solution.py:163
  357.0 5.0 fusion.4
  362.1 1.4 slice.79
  363.5 0.7 copy-done.3
  364.2 0.9 copy.43
  365.2 3.2 copy.45
  368.3 1.1 copy.44
  369.5 2.4 subtract_convert_fusion
  371.8 1.2 multiply_subtract_fusion
  373.1 7.4 %fusion.59 = (f32[4,2,512]{2,1,0:T(2,128)S(1)}, f32[4,2,512,512]{2,3,1,0:T(8,128)}) fusion(pred[512,512]{0,1:T(8,128)(4,1)} %fusion.21, bf16[512,4,2,48]{0,3,2,1:T(8,128)(2,1)} %bitcast.153, bf16[512,4,2,48]{0,3,2,1:T(8,128)(2,1)S(1)} %bitcast.152, bf16[512,4,48]{0,2,1:T(8,128)(2,1)S(1)} %get-tuple-element.11, bf16[512,4,48]{0,2,1:T(8,128)(2,1)S(1)} %get-tuple-element.10), kind=kOutput, calls=%fused_computation.123 | convolution fusion | flops 413401600 | bytes 9846784 | tf_op jit(solution)/shard_map/sub | solution.py:96
  380.5 4.2 fusion.20
  384.7 2.6 convolution_convert_fusion.1
  387.6 55.3 %all-reduce.3.cloned.1.call-done = bf16[512,1536]{1,0:T(8,128)(2,1)} async-done(((bf16[512,1536]{1,0:T(8,128)(2,1)}), bf16[512,1536]{1,0:T(8,128)(2,1)}) %all-reduce.3.cloned.1.call-update) | async-done | bytes 1572880 | tf_op jit(solution)/shard_map/psum | solution.py:184
  442.9 2.6 multiply_reduce_fusion
  445.7 12.0 %fusion.1 = f32[512,4096]{1,0:T(8,128)} fusion(bf16[1536,5632]{1,0:T(8,128)(2,1)} %bitcast.40, bf16[512,1536]{1,0:T(8,128)(2,1)S(1)} %copy-done.2, bf16[512,1536]{1,0:T(8,128)(2,1)S(1)} %copy-done.1, f32[1536]{0:T(1024)S(1)} %copy-done.10, f32[512]{0:T(512)S(1)} %add_rsqrt_fusion), kind=kOutput, calls=%fused_computation.4 | convolution fusion | flops 6447169536 | bytes 24125440 | tf_op jit(solution)/shard_map/dot_general | solution.py:106
  457.7 9.1 %convolution_convert_fusion = bf16[512,1536]{1,0:T(8,128)(2,1)} fusion(bf16[2048,1536]{1,0:T(8,128)(2,1)S(1)} %bitcast.178, f32[512,4096]{1,0:T(8,128)} %fusion.1), kind=kOutput, calls=%fused_computation.27 | convolution fusion | flops 3228303360 | bytes 16252928 | tf_op jit(solution)/shard_map/dot_general | solution.py:191
  467.1 1.2 slice_bitcast_fusion
  468.3 1.0 pad_maximum_fusion.2
  469.3 49.0 %all-reduce.5.cloned.1.call-done = bf16[512,1536]{1,0:T(8,128)(2,1)} async-done(((bf16[512,1536]{1,0:T(8,128)(2,1)}), bf16[512,1536]{1,0:T(8,128)(2,1)}) %all-reduce.5.cloned.1.call-update) | async-done | bytes 1572880 | tf_op jit(solution)/shard_map/psum | solution.py:190
  518.2 4.1 add_convert_fusion
  (102 shorter events, 4.8 us)
Async XLA Ops:
  8.0 376.7 %copy-start = (bf16[768,1536]{1,0:T(8,128)(2,1)S(1)}, bf16[768,1536]{1,0:T(8,128)(2,1)}, u32[]{:S(2)}) copy-start(bf16[768,1536]{1,0:T(8,128)(2,1)} %param.16) | copy-start | bytes 7077892
  8.0 133.6 %all-gather.5.cloned.1.call-start = ((), (), s32[]{:S(2)}) async-start(), calls=%async_computation.3 | async-start | bytes 18382848 | tf_op jit(solution)/shard_map/all_gather | solution.py:162
  15.8 3.9 copy-start.8
  33.6 7.2 %collective-permute-start = (s32[1,1,32]{2,1,0:T(1,128)S(1)}, s32[1,1,32]{2,1,0:T(1,128)S(1)}, u32[]{:S(2)}, u32[]{:S(2)}) collective-permute-start(s32[1,1,32]{2,1,0:T(1,128)S(1)} %get-tuple-element.28), channel_id=1, source_target_pairs={{0,1},{1,2},{2,3},{3,4},{4,5},{5,6},{6,7},{7,8},{8,9},{9,10},{10,1... | collective-permute-start | bytes 392 | tf_op jit(solution)/shard_map/ppermute | solution.py:37
  34.1 8.0 %collective-permute-start.1 = (s32[1,1,32]{2,1,0:T(1,128)S(1)}, s32[1,1,32]{2,1,0:T(1,128)S(1)}, u32[]{:S(2)}, u32[]{:S(2)}) collective-permute-start(s32[1,1,32]{2,1,0:T(1,128)S(1)} %get-tuple-element.27), channel_id=1, source_target_pairs={{0,2},{1,3},{2,4},{3,5},{4,6},{5,7},{6,8},{7,9},{8,10},{9,11},{10,... | collective-permute-start | bytes 392 | tf_op jit(solution)/shard_map/ppermute | solution.py:37
  36.7 9.8 %collective-permute-start.2 = (s32[1,1,32]{2,1,0:T(1,128)S(1)}, s32[1,1,32]{2,1,0:T(1,128)S(1)}, u32[]{:S(2)}, u32[]{:S(2)}) collective-permute-start(s32[1,1,32]{2,1,0:T(1,128)S(1)} %get-tuple-element.26), channel_id=1, source_target_pairs={{0,3},{1,4},{2,5},{3,6},{4,7},{5,8},{6,9},{7,10},{8,11},{9,12},{10... | collective-permute-start | bytes 392 | tf_op jit(solution)/shard_map/ppermute | solution.py:37
  39.1 7.8 %collective-permute-start.3 = (s32[1,1,32]{2,1,0:T(1,128)S(1)}, s32[1,1,32]{2,1,0:T(1,128)S(1)}, u32[]{:S(2)}, u32[]{:S(2)}) collective-permute-start(s32[1,1,32]{2,1,0:T(1,128)S(1)} %get-tuple-element.25), channel_id=1, source_target_pairs={{0,4},{1,5},{2,6},{3,7},{4,8},{5,9},{6,10},{7,11},{8,12},{9,13},{1... | collective-permute-start | bytes 392 | tf_op jit(solution)/shard_map/ppermute | solution.py:37
  40.7 6.6 %collective-permute-start.4 = (s32[1,1,32]{2,1,0:T(1,128)S(1)}, s32[1,1,32]{2,1,0:T(1,128)S(1)}, u32[]{:S(2)}, u32[]{:S(2)}) collective-permute-start(s32[1,1,32]{2,1,0:T(1,128)S(1)} %get-tuple-element.24), channel_id=1, source_target_pairs={{0,5},{1,6},{2,7},{3,8},{4,9},{5,10},{6,11},{7,12},{8,13},{9,14},{... | collective-permute-start | bytes 392 | tf_op jit(solution)/shard_map/ppermute | solution.py:37
  40.8 8.9 %collective-permute-start.5 = (s32[1,1,32]{2,1,0:T(1,128)S(1)}, s32[1,1,32]{2,1,0:T(1,128)S(1)}, u32[]{:S(2)}, u32[]{:S(2)}) collective-permute-start(s32[1,1,32]{2,1,0:T(1,128)S(1)} %get-tuple-element.23), channel_id=1, source_target_pairs={{0,6},{1,7},{2,8},{3,9},{4,10},{5,11},{6,12},{7,13},{8,14},{9,15},... | collective-permute-start | bytes 392 | tf_op jit(solution)/shard_map/ppermute | solution.py:37
  42.1 10.6 %collective-permute-start.6 = (s32[1,1,32]{2,1,0:T(1,128)S(1)}, s32[1,1,32]{2,1,0:T(1,128)S(1)}, u32[]{:S(2)}, u32[]{:S(2)}) collective-permute-start(s32[1,1,32]{2,1,0:T(1,128)S(1)} %get-tuple-element.22), channel_id=1, source_target_pairs={{0,7},{1,8},{2,9},{3,10},{4,11},{5,12},{6,13},{7,14},{8,15},{9,0},... | collective-permute-start | bytes 392 | tf_op jit(solution)/shard_map/ppermute | solution.py:37
  46.5 8.1 %collective-permute-start.7 = (s32[1,1,32]{2,1,0:T(1,128)S(1)}, s32[1,1,32]{2,1,0:T(1,128)S(1)}, u32[]{:S(2)}, u32[]{:S(2)}) collective-permute-start(s32[1,1,32]{2,1,0:T(1,128)S(1)} %get-tuple-element.21), channel_id=1, source_target_pairs={{0,8},{1,9},{2,10},{3,11},{4,12},{5,13},{6,14},{7,15},{8,0},{9,1},... | collective-permute-start | bytes 392 | tf_op jit(solution)/shard_map/ppermute | solution.py:37
  46.9 7.8 %collective-permute-start.8 = (s32[1,1,32]{2,1,0:T(1,128)S(1)}, s32[1,1,32]{2,1,0:T(1,128)S(1)}, u32[]{:S(2)}, u32[]{:S(2)}) collective-permute-start(s32[1,1,32]{2,1,0:T(1,128)S(1)} %get-tuple-element.20), channel_id=1, source_target_pairs={{0,9},{1,10},{2,11},{3,12},{4,13},{5,14},{6,15},{7,0},{8,1},{9,2},... | collective-permute-start | bytes 392 | tf_op jit(solution)/shard_map/ppermute | solution.py:37
  47.3 8.9 %collective-permute-start.9 = (s32[1,1,32]{2,1,0:T(1,128)S(1)}, s32[1,1,32]{2,1,0:T(1,128)S(1)}, u32[]{:S(2)}, u32[]{:S(2)}) collective-permute-start(s32[1,1,32]{2,1,0:T(1,128)S(1)} %get-tuple-element.19), channel_id=1, source_target_pairs={{0,10},{1,11},{2,12},{3,13},{4,14},{5,15},{6,0},{7,1},{8,2},{9,3},... | collective-permute-start | bytes 392 | tf_op jit(solution)/shard_map/ppermute | solution.py:37
  49.7 8.8 %collective-permute-start.10 = (s32[1,1,32]{2,1,0:T(1,128)S(1)}, s32[1,1,32]{2,1,0:T(1,128)S(1)}, u32[]{:S(2)}, u32[]{:S(2)}) collective-permute-start(s32[1,1,32]{2,1,0:T(1,128)S(1)} %get-tuple-element.18), channel_id=1, source_target_pairs={{0,11},{1,12},{2,13},{3,14},{4,15},{5,0},{6,1},{7,2},{8,3},{9,4},{... | collective-permute-start | bytes 392 | tf_op jit(solution)/shard_map/ppermute | solution.py:37
  52.7 5.8 %collective-permute-start.11 = (s32[1,1,32]{2,1,0:T(1,128)S(1)}, s32[1,1,32]{2,1,0:T(1,128)S(1)}, u32[]{:S(2)}, u32[]{:S(2)}) collective-permute-start(s32[1,1,32]{2,1,0:T(1,128)S(1)} %get-tuple-element.17), channel_id=1, source_target_pairs={{0,12},{1,13},{2,14},{3,15},{4,0},{5,1},{6,2},{7,3},{8,4},{9,5},{1... | collective-permute-start | bytes 392 | tf_op jit(solution)/shard_map/ppermute | solution.py:37
  54.6 4.0 collective-permute-start.12
  54.7 3.9 collective-permute-start.13
  56.2 3.6 collective-permute-start.14
  141.7 215.3 %all-to-all-start.1 = ((bf16[768,2,5632]{2,0,1:T(8,128)(2,1)}), bf16[768,2,5632]{2,0,1:T(8,128)(2,1)}, u32[]{:S(2)}, u32[]{:S(2)}) async-start(bf16[768,2,5632]{2,0,1:T(8,128)(2,1)} %all-gather.5.cloned.1.call-done), calls=%async_computation.1 | async-start | bytes 34603008 | tf_op jit(solution)/shard_map/all_to_all | solution.py:163
  151.6 54.5 %all-gather.3.cloned.1.call-start = ((), (), s32[]{:S(2)}) async-start(), calls=%async_computation.2 | async-start | bytes 2359296 | tf_op jit(solution)/shard_map/all_gather | solution.py:141
  151.8 4.8 copy-start.11
  151.8 5.0 copy-start.7
  151.8 205.1 %copy-start.9 = (f32[1536]{0:T(1024)S(1)}, f32[1536]{0:T(1024)}, u32[]{:S(2)}) copy-start(f32[1536]{0:T(1024)} %param.14) | copy-start | bytes 18436
  156.5 286.4 %all-reduce.3.cloned.1.call-start = ((), (), s32[]{:S(2)}) async-start(), calls=%async_computation.4 | async-start | bytes 3145728 | tf_op jit(solution)/shard_map/psum | solution.py:184
  362.0 2.2 copy-start.3
  364.2 4.1 slice-start
  365.2 4.3 copy-start.4
  365.2 4.3 copy-start.5
  373.1 7.4 %copy-start.6 = (bf16[512,384]{0,1:T(8,128)(2,1)S(1)}, bf16[512,384]{0,1:T(8,128)(2,1)}, u32[]{:S(2)}) copy-start(bf16[512,384]{0,1:T(8,128)(2,1)} %copy.43) | copy-start | bytes 1179652
  387.3 58.2 %copy-start.10 = (f32[1536]{0:T(1024)S(1)}, f32[1536]{0:T(1024)}, u32[]{:S(2)}) copy-start(f32[1536]{0:T(1024)} %param.17) | copy-start | bytes 18436
  387.3 130.9 %all-reduce.5.cloned.1.call-start = ((), (), s32[]{:S(2)}) async-start(), calls=%async_computation.5 | async-start | bytes 3145728 | tf_op jit(solution)/shard_map/psum | solution.py:190
  442.9 2.6 copy-start.1
  442.9 2.8 copy-start.2
  442.9 14.8 %slice-start.1 = ((s8[6291456]{0:T(1024)(128)(4,1)}), s8[4194304]{0:T(1024)(128)(4,1)S(1)}, s32[]{:S(2)}) async-start(s8[6291456]{0:T(1024)(128)(4,1)} %bitcast.177), calls=%async_computation.7 | async-start | bytes 8388608
  445.7 12.0 %slice-start.2 = ((s8[6291456]{0:T(1024)(128)(4,1)}), s8[2097152]{0:T(1024)(128)(4,1)S(1)}, s32[]{:S(2)}) async-start(s8[6291456]{0:T(1024)(128)(4,1)} %bitcast.177), calls=%async_computation.8 | async-start | bytes 4194304
Sparse Core Ops, SparseCore 0:
  19.6 122.0 all-gather.4
Sparse Core Ops, SparseCore 1:
  156.6 49.4 all-gather.2
  387.4 55.4 all-reduce.2
  467.0 51.2 all-reduce.4
